TPU v7x, 512 devices: a whole 4x4x16 slice. The times are simulated.
512 devices in a mesh: seq: 64 (over y, z), tp: 8 (over x, core).
Axes of the slice: x: 4, y: 4, z: 16, core: 2. Of those that a mesh axis runs over, the one named last changes fastest.
Arguments:
- crop_features: bfloat16 [192, 21, 21, 1536], P('seq'), may hold values from -45 to 45
- crop_counts: int32 [64], replicated, may hold values from 1 to 3, as said below
- first_crop: int32 [64], replicated, may hold values from 0 to 127, as said below
- tile_embed: bfloat16 [3, 1536], replicated, may hold values from -3 to 3
- dw_weight: bfloat16 [49, 1536], replicated, may hold values from -0.875 to 0.875
- conv_bias: bfloat16 [1536], replicated, may hold values from -3 to 3
- ln_gain: bfloat16 [1536], replicated, may hold values from 0.099609375 to 1.8984375
- ln_bias: bfloat16 [1536], replicated, may hold values from -2 to 2
- w_up: bfloat16 [1536, 6144], P('seq', 'tp'), may hold values from -0.15625 to 0.15625
- b_up: bfloat16 [6144], P('tp'), may hold values from -3 to 3
- w_down: bfloat16 [6144, 1536], P('tp', 'seq'), may hold values from -0.078125 to 0.078125
- b_down: bfloat16 [1536], P('tp'), may hold values from -2 to 2
- gamma: float32 [1536], P('tp'), may hold values from 0.5 to 2
Outputs:
- visual_rows: bfloat16 [128, 21, 21, 1536], P('seq', None, None, 'tp')
Inputs may be any that keep to these rules, and one draw needn't show every extreme that they name: `crop_counts`: the counts sum to 128; 3 is reached in every draw. first_crop[0] is 0 and the entries never fall; device d holds first_crop[d+1] - first_crop[d] crops (the last device 128 - first_crop[last]), at most 3, and some device holds exactly 3; |first_crop[d] - d * 2| <= 1.
All inputs are finite; a program needn't handle non-finite values.
Results may differ from a plain program's by a relative error of at most 0.009.
Values may be sent and summed in bfloat16 or wider, within the bound.
No kernel may reach another device: no remote copies, remote signals or barrier semaphores. Data moves between devices by JAX's collectives and lax.ppermute only.
A program may use at most 128 MiB of HBM per device.

v0:
```python
import jax
import jax.numpy as jnp
from jax import lax
from jax.sharding import PartitionSpec as P

CROPS_DEV = 2


def from_behind(block, axis, distance):
    devices = range(lax.axis_size(axis))
    route = [(i - distance, i) for i in devices if i - distance in devices]
    return lax.ppermute(block, axis, route)


def regroup(slot_data, seq_index, first_held, held_limit, per_dev):

    def outgoing(offset_dev):
        target = (seq_index + offset_dev) * per_dev + jnp.arange(per_dev, dtype=jnp.int32)
        slot_idx = jnp.clip(target - first_held, 0, slot_data.shape[0] - 1)
        is_valid = (target >= first_held) & (target < held_limit)
        picked = jnp.take(slot_data, slot_idx, axis=0)
        return jnp.where(is_valid[:, None, None, None], picked, jnp.zeros_like(picked))

    result = outgoing(0)
    for offset_dev in (1, -1):
        result = result + from_behind(outgoing(offset_dev), "seq", offset_dev)
    return result


def encode(
    block_data,
    crop_ids,
    crop_counts,
    tile_embed,
    dw_weight,
    conv_bias,
    ln_gain,
    ln_bias,
    w_up,
    b_up,
    w_down,
    b_down,
    gamma,
):
    crop_number = block_data.shape[0]
    grid_size = block_data.shape[1]
    channels = block_data.shape[3]
    kernel_side = 7
    image_start = jnp.cumsum(crop_counts) - crop_counts
    image_begin = jnp.max(
        jnp.where(image_start[None, :] <= crop_ids[:, None], image_start[None, :], 0), axis=1
    )
    place_ids = crop_ids - image_begin
    choose = (
        place_ids[:, None] == jnp.arange(tile_embed.shape[0], dtype=jnp.int32)[None, :]
    ).astype(jnp.float32)
    tile_rows = jnp.sum(choose[:, :, None] * tile_embed.astype(jnp.float32)[None, :, :], axis=1)
    block_in = block_data.astype(jnp.float32) + tile_rows[:, None, None, :]
    padded = jnp.pad(block_in, ((0, 0), (3, 3), (3, 3), (0, 0)))
    conv_sum = jnp.zeros_like(block_in)
    for row_shift in range(kernel_side):
        for col_shift in range(kernel_side):
            conv_sum = conv_sum + padded[
                :, row_shift : row_shift + grid_size, col_shift : col_shift + grid_size, :
            ] * dw_weight[row_shift * kernel_side + col_shift].astype(jnp.float32)
    cell_rows = crop_number * grid_size * grid_size
    conv_out = (conv_sum + conv_bias.astype(jnp.float32)).reshape(cell_rows, channels)
    ln_mean = jnp.mean(conv_out, axis=1, keepdims=True)
    ln_var = jnp.mean((conv_out - ln_mean) ** 2, axis=1, keepdims=True)
    normed = (
        (conv_out - ln_mean) / jnp.sqrt(ln_var + 1e-06) * ln_gain.astype(jnp.float32)
        + ln_bias.astype(jnp.float32)
    ).astype(jnp.bfloat16)
    up_whole, down_whole = (
        lax.all_gather(w_up, "seq", axis=0, tiled=True),
        lax.all_gather(w_down, "seq", axis=1, tiled=True),
    )
    pre_act = jnp.dot(normed, up_whole, preferred_element_type=jnp.float32)
    hidden = jax.nn.gelu(pre_act + b_up.astype(jnp.float32), approximate=False).astype(jnp.bfloat16)
    partial_value = jnp.dot(hidden, down_whole, preferred_element_type=jnp.float32)
    summed = lax.psum_scatter(
        partial_value.astype(jnp.bfloat16), "tp", scatter_dimension=1, tiled=True
    ).astype(jnp.float32)
    out_width = b_down.shape[0]
    offset = lax.axis_index("tp") * out_width
    residual = lax.dynamic_slice_in_dim(block_in.reshape(cell_rows, channels), offset, out_width, 1)
    result = residual + gamma * (summed + b_down.astype(jnp.float32))
    return result.astype(jnp.bfloat16).reshape(crop_number, grid_size, grid_size, out_width)


def per_device(
    crop_features,
    crop_counts,
    first_crop,
    tile_embed,
    dw_weight,
    conv_bias,
    ln_gain,
    ln_bias,
    w_up,
    b_up,
    w_down,
    b_down,
    gamma,
):
    seq_count = lax.axis_size("seq")
    seq_index = lax.axis_index("seq")
    per_dev = CROPS_DEV
    slot_count = crop_features.shape[0]
    crop_total = per_dev * seq_count
    first_held = lax.dynamic_index_in_dim(first_crop, seq_index, 0, keepdims=False)
    next_first = lax.dynamic_index_in_dim(
        first_crop, jnp.minimum(seq_index + 1, seq_count - 1), 0, keepdims=False
    )
    held_limit = jnp.where(seq_index + 1 < seq_count, next_first, crop_total)
    held_ids = first_held + jnp.arange(slot_count, dtype=jnp.int32)
    encoded = encode(
        crop_features,
        held_ids,
        crop_counts,
        tile_embed,
        dw_weight,
        conv_bias,
        ln_gain,
        ln_bias,
        w_up,
        b_up,
        w_down,
        b_down,
        gamma,
    )
    visual_rows = regroup(encoded, seq_index, first_held, held_limit, per_dev)
    return visual_rows


def solution(mesh):
    placed = (
        P("seq", None, None, None),
        P(),
        P(),
        P(),
        P(),
        P(),
        P(),
        P(),
        P("seq", "tp"),
        P("tp"),
        P("tp", "seq"),
        P("tp"),
        P("tp"),
    )
    return jax.shard_map(
        per_device,
        mesh=mesh,
        in_specs=placed,
        out_specs=P("seq", None, None, "tp"),
        check_vma=False,
    )
```

profile of v0, /device:TPU:31, one launch (start us, length us, event | category | flops | bytes accessed | tf_op | source)
XLA Modules:
  0.0 392.1 jit_solution(10020580241406690454)
XLA Ops:
  6.5 0.7 all-gather.5.cloned.1.call-update
  7.3 0.7 all-gather.3.cloned.1.call-update
  8.1 1.2 convert_reduce_fusion.46
  9.3 1.6 convert_reduce_fusion.48
  10.9 1.6 convert_reduce_fusion.47
  12.5 0.7 convert_element_type.537
  13.2 0.7 copy.20
  14.2 0.7 sub.39
  14.8 1.3 fusion.144
  17.5 0.7 convert_element_type.636
  18.3 7.2 %convert_add_fusion = f32[3,21,21,1536]{3,2,1,0:T(8,128)} fusion(bf16[3,21,21,1536]{3,2,1,0:T(8,128)(2,1)} %param.15, f32[3,1536]{1,0:T(4,128)S(1)} %multiply_reduce_fusion.1), kind=kLoop, calls=%fused_computation.149 | loop fusion | flops 4064256 | bytes 12211200 | tf_op jit(solution)/shard_map/add | solution.py:58
  25.5 179.8 %fusion.142 = (f32[3,21,21]{2,1,0:T(8,128)S(1)}, f32[3,21,21,1536]{3,2,1,0:T(8,128)}) fusion(f32[1536]{0:T(1024)S(1)} %convert_element_type.636, f32[1536]{0:T(1024)S(1)} %get-tuple-element.53, f32[1536]{0:T(1024)S(1)} %get-tuple-element.54, f32[1536]{0:T(1024)S(1)} %get-tuple-element.7, f32[1536]{0:T(1024)S(1)} %get-tuple-element.8, ...), kind=kLoop, calls=%fused_computation.281 | loop fusion | flops 201179344 | bytes 16569516 | tf_op jit(solution)/shard_map/reduce_sum | solution.py:68
  205.3 9.4 %reshape.478 = f32[1323,1536]{1,0:T(8,128)} reshape(f32[3,21,21,1536]{3,2,1,0:T(8,128)} %get-tuple-element.62) | data formatting | bytes 16257024 | tf_op jit(solution)/shard_map/reshape | solution.py:67
  215.0 4.8 %multiply_reduce_fusion = f32[3,21,21]{2,1,0:T(8,128)S(1)} fusion(f32[3,21,21,1536]{3,2,1,0:T(8,128)} %get-tuple-element.62, f32[3,21,21]{2,1,0:T(8,128)S(1)} %broadcast_multiply_fusion), kind=kLoop, calls=%fused_computation.148 | loop fusion | flops 6095061 | bytes 8139096 | tf_op jit(solution)/shard_map/reduce_sum | solution.py:69
  220.0 66.0 %all-gather.3.cloned.1.call-done = bf16[1536,768]{1,0:T(8,128)(2,1)} async-done(((bf16[24,768]{1,0:T(8,128)(2,1)}), bf16[1536,768]{1,0:T(8,128)(2,1)}) %all-gather.3.cloned.1.call-update) | async-done | bytes 2359312 | tf_op jit(solution)/shard_map/all_gather | solution.py:75
  285.9 21.7 %convolution_convert_fusion = bf16[1323,1536]{0,1:T(8,128)(2,1)} fusion(bf16[768,1536]{0,1:T(8,128)(2,1)} %all-gather.5.cloned.1.call-done, bf16[1536,768]{1,0:T(8,128)(2,1)} %all-gather.3.cloned.1.call-done, f32[1323,1536]{1,0:T(8,128)} %reshape.478, f32[1536]{0:T(1024)S(1)} %convert_element_type.638, f32[1536]{0:T(1024)S(1)} %convert_element_type.637, ...), kind=kOutput, calls=%fused_computation.151 | convolution fusion | flops 6321950208 | bytes 16937304 | tf_op jit(solution)/shard_map/dot_general | solution.py:80
  307.7 9.4 %reshape.477 = f32[1323,1536]{1,0:T(8,128)} reshape(f32[3,21,21,1536]{3,2,1,0:T(8,128)} %convert_add_fusion) | data formatting | bytes 16257024 | tf_op jit(solution)/shard_map/reshape | solution.py:86
  317.0 1.7 constant_dynamic-slice_fusion
  319.9 0.6 compare_and_fusion.4
  320.4 0.6 compare_and_fusion.1
  321.0 0.6 compare_and_fusion
  321.6 36.5 %reduce-scatter.2.cloned.1.call-done = bf16[1323,192]{0,1:T(8,128)(2,1)} async-done(((bf16[1323,1536]{0,1:T(8,128)(2,1)}), bf16[1323,192]{0,1:T(8,128)(2,1)}) %reduce-scatter.2.cloned.1.call-update) | async-done | bytes 508048 | tf_op jit(solution)/shard_map/reduce_scatter | solution.py:81
  358.1 1.4 add_convert_fusion.6
  360.1 0.6 gather_fusion.2
  360.8 6.0 %collective-permute-start.1 = (bf16[2,21,21,192]{3,2,1,0:T(8,128)(2,1)S(1)}, bf16[2,21,21,192]{3,2,1,0:T(8,128)(2,1)S(1)}, u32[]{:S(2)}, u32[]{:S(2)}) collective-permute-start(bf16[2,21,21,192]{3,2,1,0:T(8,128)(2,1)S(1)} %select_select_fusion), channel_id=1, source_target_pairs={{8,0},{16,8},{24,16},{32,24},{40,32},{48,40},{56,48},{64,56},{72,6... | collective-permute-start | bytes 1016072 | tf_op jit(solution)/shard_map/ppermute | solution.py:12
  366.8 0.6 gather_fusion.1
  367.5 1.9 collective-permute-start
  369.4 0.6 compare_and_fusion.2
  370.0 0.6 gather_fusion
  370.6 6.8 %collective-permute-done.1 = bf16[2,21,21,192]{3,2,1,0:T(8,128)(2,1)S(1)} collective-permute-done((bf16[2,21,21,192]{3,2,1,0:T(8,128)(2,1)S(1)}, bf16[2,21,21,192]{3,2,1,0:T(8,128)(2,1)S(1)}, u32[]{:S(2)}, u32[]{:S(2)}) %collective-permute-start.1) | collective-permute-done | bytes 338720 | tf_op jit(solution)/shard_map/ppermute | solution.py:12
  377.4 6.9 %collective-permute-done = bf16[2,21,21,192]{3,2,1,0:T(8,128)(2,1)S(1)} collective-permute-done((bf16[2,21,21,192]{3,2,1,0:T(8,128)(2,1)S(1)}, bf16[2,21,21,192]{3,2,1,0:T(8,128)(2,1)S(1)}, u32[]{:S(2)}, u32[]{:S(2)}) %collective-permute-start) | collective-permute-done | bytes 338720 | tf_op jit(solution)/shard_map/ppermute | solution.py:12
  384.5 1.1 copy.23
  (39 shorter events, 3.6 us)
Async XLA Ops:
  6.5 213.4 %all-gather.5.cloned.1.call-start = ((), (), s32[]{:S(2)}) async-start(), calls=%async_computation.2 | async-start | bytes 2396160 | tf_op jit(solution)/shard_map/all_gather | solution.py:76
  7.3 278.7 %all-gather.3.cloned.1.call-start = ((), (), s32[]{:S(2)}) async-start(), calls=%async_computation.1 | async-start | bytes 2396160 | tf_op jit(solution)/shard_map/all_gather | solution.py:75
  8.0 350.1 %reduce-scatter.2.cloned.1.call-start = ((), (), s32[]{:S(2)}) async-start(), calls=%async_computation.3 | async-start | bytes 4866048 | tf_op jit(solution)/shard_map/reduce_scatter | solution.py:81
  205.3 9.5 %copy-start = (bf16[1536]{0:T(1024)(128)(2,1)S(1)}, bf16[1536]{0:T(1024)(128)(2,1)}, u32[]{:S(2)}) copy-start(bf16[1536]{0:T(1024)(128)(2,1)} %param.22) | copy-start | bytes 9220
  205.3 9.5 %copy-start.1 = (bf16[1536]{0:T(1024)(128)(2,1)S(1)}, bf16[1536]{0:T(1024)(128)(2,1)}, u32[]{:S(2)}) copy-start(bf16[1536]{0:T(1024)(128)(2,1)} %param.21) | copy-start | bytes 9220
  205.3 14.6 %copy-start.2 = (bf16[768]{0:T(1024)(128)(2,1)S(1)}, bf16[768]{0:T(1024)(128)(2,1)}, u32[]{:S(2)}) copy-start(bf16[768]{0:T(1024)(128)(2,1)} %param.24) | copy-start | bytes 4612
  307.6 11.6 %copy-start.4 = (bf16[192]{0:T(256)(128)(2,1)S(1)}, bf16[192]{0:T(256)(128)(2,1)}, u32[]{:S(2)}) copy-start(bf16[192]{0:T(256)(128)(2,1)} %param.26) | copy-start | bytes 1156
  307.6 50.4 %copy-start.3 = (f32[192]{0:T(256)S(1)}, f32[192]{0:T(256)}, u32[]{:S(2)}) copy-start(f32[192]{0:T(256)} %param.27) | copy-start | bytes 2308
  360.8 16.6 %collective-permute-start.1 = (bf16[2,21,21,192]{3,2,1,0:T(8,128)(2,1)S(1)}, bf16[2,21,21,192]{3,2,1,0:T(8,128)(2,1)S(1)}, u32[]{:S(2)}, u32[]{:S(2)}) collective-permute-start(bf16[2,21,21,192]{3,2,1,0:T(8,128)(2,1)S(1)} %select_select_fusion), channel_id=1, source_target_pairs={{8,0},{16,8},{24,16},{32,24},{40,32},{48,40},{56,48},{64,56},{72,6... | collective-permute-start | bytes 1016072 | tf_op jit(solution)/shard_map/ppermute | solution.py:12
  367.5 16.8 %collective-permute-start = (bf16[2,21,21,192]{3,2,1,0:T(8,128)(2,1)S(1)}, bf16[2,21,21,192]{3,2,1,0:T(8,128)(2,1)S(1)}, u32[]{:S(2)}, u32[]{:S(2)}) collective-permute-start(bf16[2,21,21,192]{3,2,1,0:T(8,128)(2,1)S(1)} %select_select_fusion.1), channel_id=1, source_target_pairs={{0,8},{8,16},{16,24},{24,32},{32,40},{40,48},{48,56},{56,64},{64,7... | collective-permute-start | bytes 1016072 | tf_op jit(solution)/shard_map/ppermute | solution.py:12
Sparse Core Ops, SparseCore 0:
  10.3 135.3 all-gather.4
  148.7 137.1 all-gather.2
  307.8 50.2 reduce-scatter.1
where the time goes:
time: 393 us; the launch traced here: 392 us
  other arithmetic  204 us (52%)
  waiting for transfers between devices  118 us (30%)
  local copies, waits for them, and re-layouts  26.8 us (7%)
  matrix products  21.7 us (6%)
  between operations  14.1 us (4%)
  starting transfers between devices  7.98 us (2%)
    reduce_sum x1, other arithmetic, encode(): ln_mean = jnp.mean(conv_out, axis=1, keepdims=True)  180 us
    all_gather x1, waiting for transfers between devices, encode(): lax.all_gather(w_up, 'seq', axis=0, tiled=True)  66 us
    reduce_scatter x1, waiting for transfers between devices, encode(): lax.psum_scatter(partial_value.astype(jnp.bfloat16), 'tp', scatter_dimens...  36.5 us
    dot_general x1, matrix products, encode(): jnp.dot(hidden, down_whole, preferred_element_type=jnp.float32)  21.7 us
    ppermute x2, waiting for transfers between devices, from_behind(): return lax.ppermute(block, axis, route)  13.7 us
    reshape x1, local copies, waits for them, and re-layouts, encode(): (conv_sum + conv_bias.astype(jnp.float32)).reshape(cell_rows, channels)  9.45 us
    reshape x1, local copies, waits for them, and re-layouts, encode(): block_in.reshape(cell_rows, channels)  9.35 us
    ppermute x2, starting transfers between devices, from_behind(): return lax.ppermute(block, axis, route)  7.9 us
  transfers between devices with their start and end apart: 5, of which 4 were waited for; matrix products, arithmetic and copies ran while one was open for 58% of the time, Pallas kernels for 0%

commit v1 on v0

--- a/solution.py
+++ b/solution.py
@@ -72,7 +72,9 @@
         + ln_bias.astype(jnp.float32)
     ).astype(jnp.bfloat16)
     up_whole, down_whole = (
-        lax.all_gather(w_up, "seq", axis=0, tiled=True),
+        jnp.concatenate(
+            lax.all_to_all(jnp.stack([w_up] * lax.axis_size("seq")), "seq", 0, 0), axis=0
+        ),
         lax.all_gather(w_down, "seq", axis=1, tiled=True),
     )
     pre_act = jnp.dot(normed, up_whole, preferred_element_type=jnp.float32)

time: 393 us -> 343 us (0.87)
  waiting for transfers between devices: 118 us -> 45.5 us
  starting transfers between devices: 7.98 us -> 26 us
  other arithmetic: 204 us -> 208 us
    all_gather x1 -> x0, waiting for transfers between devices: 66 us -> none  [encode(): lax.all_gather(w_up, 'seq', axis=0, tiled=True)]
    all_to_all x0 -> x1, starting transfers between devices: none -> 18.1 us  [encode(): lax.all_to_all(jnp.stack([w_up] * lax.axis_size('seq')), 'seq', 0, 0)]
    reshape x1 -> x0, local copies, waits for them, and re-layouts: 9.45 us -> none  [encode(): (conv_sum + conv_bias.astype(jnp.float32)).reshape(cell_rows, channels)]
    convert_element_type x0 -> x1, local copies, waits for them, and re-layouts: none -> 7.22 us  [encode(): normed = ((conv_out - ln_mean) / jnp.sqrt(ln_var + 1e-06) * ln_gain.astyp...]
    reduce_scatter x1, waiting for transfers between devices: 36.5 us -> 31.2 us  [encode(): lax.psum_scatter(partial_value.astype(jnp.bfloat16), 'tp', scatter_dimens...]
  transfers between devices with their start and end apart: 5 -> 5, of which waited for: 4 -> 3; matrix products, arithmetic and copies ran while one was open for 58% -> 68% of each run, Pallas kernels for 0% -> 0%
where the time goes in v1:
time: 343 us; the launch traced here: 341 us
  other arithmetic  208 us (61%)
  waiting for transfers between devices  45.5 us (13%)
  local copies, waits for them, and re-layouts  28.1 us (8%)
  starting transfers between devices  26 us (8%)
  matrix products  19.1 us (6%)
  between operations  14.3 us (4%)
    reduce_sum x1, other arithmetic, encode(): ln_mean = jnp.mean(conv_out, axis=1, keepdims=True)  179 us
    reduce_scatter x1, waiting for transfers between devices, encode(): lax.psum_scatter(partial_value.astype(jnp.bfloat16), 'tp', scatter_dimens...  31.2 us
    dot_general x1, matrix products, encode(): jnp.dot(hidden, down_whole, preferred_element_type=jnp.float32)  19.1 us
    all_to_all x1, starting transfers between devices, encode(): lax.all_to_all(jnp.stack([w_up] * lax.axis_size('seq')), 'seq', 0, 0)  18.1 us
    ppermute x2, waiting for transfers between devices, from_behind(): return lax.ppermute(block, axis, route)  13.5 us
    reshape x1, local copies, waits for them, and re-layouts, encode(): block_in.reshape(cell_rows, channels)  9.41 us
    ppermute x2, starting transfers between devices, from_behind(): return lax.ppermute(block, axis, route)  7.83 us
    convert_element_type x1, local copies, waits for them, and re-layouts, encode(): normed = ((conv_out - ln_mean) / jnp.sqrt(ln_var + 1e-06) * ln_gain.astyp...  7.22 us
  transfers between devices with their start and end apart: 5, of which 3 were waited for; matrix products, arithmetic and copies ran while one was open for 68% of the time, Pallas kernels for 0%

profile of v1, /device:TPU:31, one launch (start us, length us, event | category | flops | bytes accessed | tf_op | source)
XLA Modules:
  0.0 341.3 jit_solution(9310153967586162304)
XLA Ops:
  6.5 0.7 all-gather.2.cloned.1.call-update
  7.3 2.4 stack.2
  9.7 18.1 %all-to-all-start = ((bf16[64,24,768]{2,1,0:T(8,128)(2,1)}), bf16[64,24,768]{2,1,0:T(8,128)(2,1)S(1)}, u32[]{:S(2)}, u32[]{:S(2)}) async-start(bf16[64,24,768]{2,1,0:T(8,128)(2,1)} %stack.2), calls=%async_computation | async-start | bytes 4718592 | tf_op jit(solution)/shard_map/all_to_all | solution.py:76
  27.9 1.2 convert_reduce_fusion.46
  29.1 1.7 convert_reduce_fusion.48
  30.8 1.6 convert_reduce_fusion.47
  32.4 0.7 convert_element_type.540
  33.1 0.7 copy.20
  34.7 1.4 fusion.143
  36.1 0.7 iota_add_fusion.2
  37.0 0.7 fusion.140
  37.8 0.7 convert_element_type.639
  38.6 7.2 %convert_add_fusion = f32[3,21,21,1536]{3,2,1,0:T(8,128)} fusion(bf16[3,21,21,1536]{3,2,1,0:T(8,128)(2,1)} %param.15, f32[3,1536]{1,0:T(4,128)S(1)} %multiply_reduce_fusion.1), kind=kLoop, calls=%fused_computation.150 | loop fusion | flops 4064256 | bytes 12211200 | tf_op jit(solution)/shard_map/add | solution.py:58
  45.8 179.5 %fusion.141 = (f32[3,21,21]{2,1,0:T(8,128)S(1)}, f32[3,21,21,1536]{3,2,1,0:T(8,128)}) fusion(f32[1536]{0:T(1024)S(1)} %convert_element_type.639, f32[1536]{0:T(1024)S(1)} %get-tuple-element.53, f32[1536]{0:T(1024)S(1)} %get-tuple-element.54, f32[1536]{0:T(1024)S(1)} %get-tuple-element.7, f32[1536]{0:T(1024)S(1)} %get-tuple-element.8, ...), kind=kLoop, calls=%fused_computation.280 | loop fusion | flops 201179344 | bytes 16569516 | tf_op jit(solution)/shard_map/reduce_sum | solution.py:68
  225.4 4.9 %multiply_reduce_fusion = f32[3,21,21]{2,1,0:T(8,128)S(1)} fusion(f32[3,21,21,1536]{3,2,1,0:T(8,128)} %get-tuple-element.62, f32[3,21,21]{2,1,0:T(8,128)S(1)} %broadcast_multiply_fusion), kind=kLoop, calls=%fused_computation.149 | loop fusion | flops 6095061 | bytes 8139096 | tf_op jit(solution)/shard_map/reduce_sum | solution.py:69
  230.3 1.3 copy-done
  231.6 3.4 add_convert_fusion
  235.0 7.2 %convert_element_type.643 = bf16[1323,1536]{1,0:T(8,128)(2,1)} reshape(bf16[3,21,21,1536]{3,2,1,0:T(8,128)(2,1)} %add_convert_fusion) | data formatting | bytes 8128512 | tf_op jit(solution)/shard_map/convert_element_type | solution.py:73
  242.2 19.1 %convolution_convert_fusion = bf16[1323,1536]{0,1:T(8,128)(2,1)} fusion(bf16[768,1536]{0,1:T(8,128)(2,1)} %all-gather.2.cloned.1.call-done, bf16[1323,1536]{1,0:T(8,128)(2,1)} %convert_element_type.643, bf16[1536,768]{1,0:T(8,128)(2,1)S(1)} %bitcast.7, f32[768]{0:T(1024)S(1)} %convert_element_type.644), kind=kOutput, calls=%fused_computation.151 | convolution fusion | flops 6311789568 | bytes 12850176 | tf_op jit(solution)/shard_map/dot_general | solution.py:82
  261.4 9.4 %reshape.492 = f32[1323,1536]{1,0:T(8,128)} reshape(f32[3,21,21,1536]{3,2,1,0:T(8,128)} %convert_add_fusion) | data formatting | bytes 16257024 | tf_op jit(solution)/shard_map/reshape | solution.py:88
  270.8 1.7 constant_dynamic-slice_fusion
  273.6 0.7 compare_and_fusion.4
  274.3 0.7 compare_and_fusion.1
  275.0 0.7 compare_and_fusion
  275.8 31.2 %reduce-scatter.2.cloned.1.call-done = bf16[1323,192]{0,1:T(8,128)(2,1)} async-done(((bf16[1323,1536]{0,1:T(8,128)(2,1)}), bf16[1323,192]{0,1:T(8,128)(2,1)}) %reduce-scatter.2.cloned.1.call-update) | async-done | bytes 508048 | tf_op jit(solution)/shard_map/reduce_scatter | solution.py:83
  307.0 1.4 add_convert_fusion.1
  309.7 5.9 %collective-permute-start.1 = (bf16[2,21,21,192]{3,2,1,0:T(8,128)(2,1)S(1)}, bf16[2,21,21,192]{3,2,1,0:T(8,128)(2,1)S(1)}, u32[]{:S(2)}, u32[]{:S(2)}) collective-permute-start(bf16[2,21,21,192]{3,2,1,0:T(8,128)(2,1)S(1)} %select_select_fusion), channel_id=1, source_target_pairs={{8,0},{16,8},{24,16},{32,24},{40,32},{48,40},{56,48},{64,56},{72,6... | collective-permute-start | bytes 1016072 | tf_op jit(solution)/shard_map/ppermute | solution.py:12
  316.4 1.9 collective-permute-start
  318.3 0.7 compare_and_fusion.2
  319.6 6.6 %collective-permute-done.1 = bf16[2,21,21,192]{3,2,1,0:T(8,128)(2,1)S(1)} collective-permute-done((bf16[2,21,21,192]{3,2,1,0:T(8,128)(2,1)S(1)}, bf16[2,21,21,192]{3,2,1,0:T(8,128)(2,1)S(1)}, u32[]{:S(2)}, u32[]{:S(2)}) %collective-permute-start.1) | collective-permute-done | bytes 338720 | tf_op jit(solution)/shard_map/ppermute | solution.py:12
  326.2 6.9 %collective-permute-done = bf16[2,21,21,192]{3,2,1,0:T(8,128)(2,1)S(1)} collective-permute-done((bf16[2,21,21,192]{3,2,1,0:T(8,128)(2,1)S(1)}, bf16[2,21,21,192]{3,2,1,0:T(8,128)(2,1)S(1)}, u32[]{:S(2)}, u32[]{:S(2)}) %collective-permute-start) | collective-permute-done | bytes 338720 | tf_op jit(solution)/shard_map/ppermute | solution.py:12
  333.3 1.1 copy.23
  (40 shorter events, 4.6 us)
Async XLA Ops:
  6.5 235.7 %all-gather.2.cloned.1.call-start = ((), (), s32[]{:S(2)}) async-start(), calls=%async_computation.2 | async-start | bytes 2396160 | tf_op jit(solution)/shard_map/all_gather | solution.py:78
  9.7 232.5 %all-to-all-start = ((bf16[64,24,768]{2,1,0:T(8,128)(2,1)}), bf16[64,24,768]{2,1,0:T(8,128)(2,1)S(1)}, u32[]{:S(2)}, u32[]{:S(2)}) async-start(bf16[64,24,768]{2,1,0:T(8,128)(2,1)} %stack.2), calls=%async_computation | async-start | bytes 4718592 | tf_op jit(solution)/shard_map/all_to_all | solution.py:76
  27.9 279.1 %reduce-scatter.2.cloned.1.call-start = ((), (), s32[]{:S(2)}) async-start(), calls=%async_computation.3 | async-start | bytes 4866048 | tf_op jit(solution)/shard_map/reduce_scatter | solution.py:83
  45.8 179.5 %copy-start.1 = (bf16[1536]{0:T(1024)(128)(2,1)S(1)}, bf16[1536]{0:T(1024)(128)(2,1)}, u32[]{:S(2)}) copy-start(bf16[1536]{0:T(1024)(128)(2,1)} %param.22) | copy-start | bytes 9220
  45.8 179.5 %copy-start.2 = (bf16[1536]{0:T(1024)(128)(2,1)S(1)}, bf16[1536]{0:T(1024)(128)(2,1)}, u32[]{:S(2)}) copy-start(bf16[1536]{0:T(1024)(128)(2,1)} %param.21) | copy-start | bytes 9220
  225.3 6.3 %copy-start = (f32[3,21,21,1536]{3,2,1,0:T(8,128)S(1)}, f32[3,21,21,1536]{3,2,1,0:T(8,128)}, u32[]{:S(2)}) copy-start(f32[3,21,21,1536]{3,2,1,0:T(8,128)} %get-tuple-element.62) | copy-start | bytes 24385540
  231.6 10.6 %copy-start.3 = (bf16[768]{0:T(1024)(128)(2,1)S(1)}, bf16[768]{0:T(1024)(128)(2,1)}, u32[]{:S(2)}) copy-start(bf16[768]{0:T(1024)(128)(2,1)} %param.24) | copy-start | bytes 4612
  261.3 11.6 %copy-start.5 = (bf16[192]{0:T(256)(128)(2,1)S(1)}, bf16[192]{0:T(256)(128)(2,1)}, u32[]{:S(2)}) copy-start(bf16[192]{0:T(256)(128)(2,1)} %param.26) | copy-start | bytes 1156
  261.4 45.6 %copy-start.4 = (f32[192]{0:T(256)S(1)}, f32[192]{0:T(256)}, u32[]{:S(2)}) copy-start(f32[192]{0:T(256)} %param.27) | copy-start | bytes 2308
  309.7 16.5 %collective-permute-start.1 = (bf16[2,21,21,192]{3,2,1,0:T(8,128)(2,1)S(1)}, bf16[2,21,21,192]{3,2,1,0:T(8,128)(2,1)S(1)}, u32[]{:S(2)}, u32[]{:S(2)}) collective-permute-start(bf16[2,21,21,192]{3,2,1,0:T(8,128)(2,1)S(1)} %select_select_fusion), channel_id=1, source_target_pairs={{8,0},{16,8},{24,16},{32,24},{40,32},{48,40},{56,48},{64,56},{72,6... | collective-permute-start | bytes 1016072 | tf_op jit(solution)/shard_map/ppermute | solution.py:12
  316.4 16.8 %collective-permute-start = (bf16[2,21,21,192]{3,2,1,0:T(8,128)(2,1)S(1)}, bf16[2,21,21,192]{3,2,1,0:T(8,128)(2,1)S(1)}, u32[]{:S(2)}, u32[]{:S(2)}) collective-permute-start(bf16[2,21,21,192]{3,2,1,0:T(8,128)(2,1)S(1)} %select_select_fusion.1), channel_id=1, source_target_pairs={{0,8},{8,16},{16,24},{24,32},{32,40},{40,48},{48,56},{56,64},{64,7... | collective-permute-start | bytes 1016072 | tf_op jit(solution)/shard_map/ppermute | solution.py:12
Sparse Core Ops, SparseCore 0:
  10.3 164.9 all-gather.1
  261.5 45.4 reduce-scatter.1
